TPU v7x, 32 devices: a whole 2x2x4 slice. The times are simulated.
32 devices in a mesh: expert: 8 (over z, core), fsdp: 4 (over y, x).
Axes of the slice: x: 2, y: 2, z: 4, core: 2. Of those that a mesh axis runs over, the one named last changes fastest.
Arguments:
- hidden_in: bfloat16 [16384, 768], P(('expert', 'fsdp')), may hold values from -6 to 6
- routes: int32 [16384, 2], P(('expert', 'fsdp')), may hold values from 0 to 7, all different within a row; in each aligned block of 512 rows (0 to 511, 512 to 1023, ...) at most 256 rows name the same one
- attn_gain: bfloat16 [768], P(('expert', 'fsdp')), may hold values from 0.25 to 1.75
- w_query: bfloat16 [768, 768], P(('expert', 'fsdp')), may hold values from -0.21875 to 0.21875
- w_key: bfloat16 [768, 768], P(('expert', 'fsdp')), may hold values from -0.21875 to 0.21875
- w_value: bfloat16 [768, 768], P(('expert', 'fsdp')), may hold values from -0.21875 to 0.21875
- w_output: bfloat16 [768, 768], P(('expert', 'fsdp')), may hold values from -1.25 to 1.25
- ffn_gain: bfloat16 [768], P(('expert', 'fsdp')), may hold values from 0.25 to 1.75
- w_router: bfloat16 [768, 8], P(('expert', 'fsdp')), may hold values from -0.21875 to 0.21875
- shared_gate: bfloat16 [768, 2048], P(('expert', 'fsdp')), may hold values from -0.21875 to 0.21875
- shared_up: bfloat16 [768, 2048], P(('expert', 'fsdp')), may hold values from -0.21875 to 0.21875
- shared_down: bfloat16 [2048, 768], P(('expert', 'fsdp')), may hold values from -0.125 to 0.125
- expert_gate: bfloat16 [8, 768, 2048], P('expert', 'fsdp'), may hold values from -0.21875 to 0.21875
- expert_up: bfloat16 [8, 768, 2048], P('expert', 'fsdp'), may hold values from -0.21875 to 0.21875
- expert_down: bfloat16 [8, 2048, 768], P('expert', 'fsdp'), may hold values from -0.125 to 0.125
- cotangent: bfloat16 [16384, 768], P(('expert', 'fsdp')), may hold values from -6 to 6
Outputs:
- hidden_out: bfloat16 [16384, 768], P(('expert', 'fsdp'))
- grad_hidden: float32 [16384, 768], P(('expert', 'fsdp'))
- grad_attn_gain: float32 [768], P(('expert', 'fsdp'))
- grad_query: float32 [768, 768], P(('expert', 'fsdp'))
- grad_key: float32 [768, 768], P(('expert', 'fsdp'))
- grad_value: float32 [768, 768], P(('expert', 'fsdp'))
- grad_output: float32 [768, 768], P(('expert', 'fsdp'))
- grad_ffn_gain: float32 [768], P(('expert', 'fsdp'))
- grad_router: float32 [768, 8], P(('expert', 'fsdp'))
- grad_shared_gate: float32 [768, 2048], P(('expert', 'fsdp'))
- grad_shared_up: float32 [768, 2048], P(('expert', 'fsdp'))
- grad_shared_down: float32 [2048, 768], P(('expert', 'fsdp'))
- grad_expert_gate: float32 [8, 768, 2048], P('expert', 'fsdp')
- expert_up_weight_gradient: float32 [8, 768, 2048], P('expert', 'fsdp')
- grad_expert_down: float32 [8, 2048, 768], P('expert', 'fsdp')
Inputs may be any that keep to these rules, and one draw needn't show every extreme that they name: `routes`: each row names 2 different experts. In the rows of one device no expert is named more than 256 times, and in every draw some device's rows name some expert exactly 256 times.
All inputs are finite; a program needn't handle non-finite values.
Results may differ from a plain program's by a relative error of at most 0.015.
Values may be sent and summed in bfloat16 or wider, within the bound.
No kernel may reach another device: no remote copies, remote signals or barrier semaphores. Data moves between devices by JAX's collectives and lax.ppermute only.
A program may use at most 256 MiB of HBM per device.

v0:
```python
import jax
import jax.numpy as jnp
from jax import lax
from jax.sharding import PartitionSpec as P

HEADS = 12
HEAD_DIM = 64
TOP = 2
BLOCK = 256


EPSILON = 1e-06
NEGATIVE = -1e30


def normalize(values, gain):
    return values * lax.rsqrt(jnp.mean(values * values, axis=-1, keepdims=True) + EPSILON) * gain


def swish(values):
    return values * jax.nn.sigmoid(values)


def gated(gate_part, up_part):
    return swish(gate_part) * up_part


def gated_gradient_rows(gate_part, up_part, inner_gradient_rows):
    unused, pullback = jax.vjp(gated, gate_part, up_part)
    return pullback(inner_gradient_rows)


def matmul(left, right):
    return jnp.dot(left, right, preferred_element_type=jnp.float32)


def multiply_transposed_left(left, right):
    return lax.dot_general(
        left, right, (((0,), (0,)), ((), ())), preferred_element_type=jnp.float32
    )


def multiply_transposed_right(left, right):
    return lax.dot_general(
        left, right, (((1,), (1,)), ((), ())), preferred_element_type=jnp.float32
    )


def rope_tables(length, head_size):
    half = head_size // 2
    freqs = jnp.exp(-jnp.log(10000.0) * jnp.arange(half, dtype=jnp.float32) * 2.0 / head_size)
    angles = jnp.arange(length, dtype=jnp.float32)[:, None] * freqs[None, :]
    return (jnp.cos(angles)[:, None, :], jnp.sin(angles)[:, None, :])


def rotate(values, cosine, sine):
    half = values.shape[-1] // 2
    first = values[..., :half]
    second = values[..., half:]
    return jnp.concatenate(
        [first * cosine - second * sine, second * cosine + first * sine], axis=-1
    )


def block_mask(first_row, block_rows, length):
    query_block = (first_row + jnp.arange(block_rows, dtype=jnp.int32)) // BLOCK
    key_block = jnp.arange(length, dtype=jnp.int32) // BLOCK
    return key_block[None, :] <= query_block[:, None]


def attend_forward(query_states, key_states, value_states, block_rows, score_scale):
    length, head_count, head_size = query_states.shape
    block_count = length // block_rows

    def one_block(block_index):
        first_row = block_index * block_rows
        scores = (
            jnp.einsum("qhd,khd->hqk", query_states, key_states, preferred_element_type=jnp.float32)
            * score_scale
        )
        scores = jnp.where(block_mask(first_row, block_rows, length)[None], scores, NEGATIVE)
        maximum = jnp.max(scores, axis=-1, keepdims=True)
        exponent = jnp.exp(scores - maximum)
        denominator = jnp.sum(exponent, axis=-1, keepdims=True)
        probability = (exponent / denominator).astype(jnp.bfloat16)
        mixture = jnp.einsum(
            "hqk,khd->qhd", probability, value_states, preferred_element_type=jnp.float32
        )
        return (mixture.astype(jnp.bfloat16), (maximum + jnp.log(denominator))[..., 0])

    mixture, log_total = lax.map(one_block, jnp.arange(block_count, dtype=jnp.int32))
    return (mixture.reshape(length, head_count * head_size), log_total)


def attend_backward(
    query_states, key_states, value_states, grad_mixture, log_total, block_rows, score_scale
):
    length, head_count, head_size = query_states.shape
    block_count = length // block_rows

    def one_block(carry, block_index):
        grad_keys, grad_values = carry
        first_row = block_index * block_rows
        scores = (
            jnp.einsum("qhd,khd->hqk", query_states, key_states, preferred_element_type=jnp.float32)
            * score_scale
        )
        scores = jnp.where(block_mask(first_row, block_rows, length)[None], scores, NEGATIVE)
        probability = jnp.exp(scores - log_total[block_index][..., None])
        grad_prob = jnp.einsum(
            "qhd,khd->hqk", grad_mixture, value_states, preferred_element_type=jnp.float32
        )
        grad_scores = (
            probability * (grad_prob - jnp.sum(probability * grad_prob, axis=-1, keepdims=True))
        ).astype(jnp.bfloat16)
        grad_query = (
            jnp.einsum("hqk,khd->qhd", grad_scores, key_states, preferred_element_type=jnp.float32)
            * score_scale
        )
        grad_keys = (
            grad_keys
            + jnp.einsum(
                "hqk,qhd->khd", grad_scores, query_states, preferred_element_type=jnp.float32
            )
            * score_scale
        )
        grad_values = grad_values + jnp.einsum(
            "hqk,qhd->khd",
            probability.astype(jnp.bfloat16),
            grad_mixture,
            preferred_element_type=jnp.float32,
        )
        return ((grad_keys, grad_values), grad_query)

    zero_states = jnp.zeros((length, head_count, head_size), jnp.float32)
    (grad_keys, grad_values), grad_query = lax.scan(
        one_block, (zero_states, zero_states), jnp.arange(block_count, dtype=jnp.int32)
    )
    return (grad_query.reshape(length, head_count, head_size), grad_keys, grad_values)


def slot_tables(routes, expert_count, capacity):
    flat = routes.reshape(-1)
    onehot = (flat[:, None] == jnp.arange(expert_count, dtype=jnp.int32)[None, :]).astype(jnp.int32)
    place = jnp.sum((jnp.cumsum(onehot, axis=0) - onehot) * onehot, axis=1)
    slots = flat * capacity + place
    owners = jnp.full((expert_count * capacity,), flat.shape[0], jnp.int32)
    owners = owners.at[slots].set(jnp.arange(flat.shape[0], dtype=jnp.int32))
    return (slots, owners)


def per_device(
    hidden_in,
    routes,
    attn_gain,
    w_query,
    w_key,
    w_value,
    w_output,
    ffn_gain,
    w_router,
    shared_gate,
    shared_up,
    shared_down,
    expert_gate,
    expert_up,
    expert_down,
    cotangent,
):
    gathered = (
        lax.all_gather(attn_gain, ("expert", "fsdp"), axis=0, tiled=True),
        lax.all_gather(w_query, ("expert", "fsdp"), axis=0, tiled=True),
        lax.all_gather(w_key, ("expert", "fsdp"), axis=0, tiled=True),
        lax.all_gather(w_value, ("expert", "fsdp"), axis=0, tiled=True),
        lax.all_gather(w_output, ("expert", "fsdp"), axis=0, tiled=True),
        lax.all_gather(ffn_gain, ("expert", "fsdp"), axis=0, tiled=True),
        lax.all_gather(w_router, ("expert", "fsdp"), axis=0, tiled=True),
        lax.all_gather(shared_gate, ("expert", "fsdp"), axis=0, tiled=True),
        lax.all_gather(shared_up, ("expert", "fsdp"), axis=0, tiled=True),
        lax.all_gather(shared_down, ("expert", "fsdp"), axis=0, tiled=True),
    )
    (
        gain_one,
        query_weight,
        key_weight,
        value_weight,
        output_weight,
        gain_two,
        router_weight,
        shared_gating,
        shared_upward,
        shared_downward,
    ) = gathered
    expert_full = (
        lax.all_gather(expert_gate, "fsdp", axis=1, tiled=True),
        lax.all_gather(expert_up, "fsdp", axis=1, tiled=True),
        lax.all_gather(expert_down, "fsdp", axis=1, tiled=True),
    )
    expert_gate_activation = expert_full[0][0]
    expert_up_projection = expert_full[1][0]
    expert_downward = expert_full[2][0]
    token_count, width = hidden_in.shape
    score_scale = HEAD_DIM ** (-0.5)
    block_rows = min(512, token_count)
    cosine, sine = rope_tables(token_count, HEAD_DIM)
    residual = hidden_in.astype(jnp.float32)
    gain_first = gain_one.astype(jnp.float32)
    normed_first = normalize(residual, gain_first).astype(jnp.bfloat16)
    query_raw = matmul(normed_first, query_weight).reshape(token_count, HEADS, HEAD_DIM)
    query_states = rotate(query_raw, cosine, sine).astype(jnp.bfloat16)
    key_raw = matmul(normed_first, key_weight).reshape(token_count, HEADS, HEAD_DIM)
    key_states = rotate(key_raw, cosine, sine).astype(jnp.bfloat16)
    value_states = (
        matmul(normed_first, value_weight)
        .astype(jnp.bfloat16)
        .reshape(token_count, HEADS, HEAD_DIM)
    )
    mixture, log_total = attend_forward(
        query_states, key_states, value_states, block_rows, score_scale
    )
    after_attn = residual + matmul(mixture, output_weight)
    gain_second = gain_two.astype(jnp.float32)
    normed_second = normalize(after_attn, gain_second).astype(jnp.bfloat16)
    logits = matmul(normed_second, router_weight)
    chosen = jnp.take_along_axis(logits, routes, axis=1)
    gates = jax.nn.softmax(chosen, axis=-1)
    shared_gate_part = matmul(normed_second, shared_gating)
    shared_up_part = matmul(normed_second, shared_upward)
    shared_inner = gated(shared_gate_part, shared_up_part).astype(jnp.bfloat16)
    shared_result = matmul(shared_inner, shared_downward)
    expert_count = router_weight.shape[1]
    capacity = 2 * TOP * token_count // expert_count
    slots, owners = slot_tables(routes, expert_count, capacity)
    owner_token = jnp.where(owners < token_count * TOP, owners // TOP, token_count)
    padded_rows = jnp.concatenate([normed_second, jnp.zeros((1, width), jnp.bfloat16)], axis=0)
    outgoing = padded_rows[owner_token].reshape(expert_count, capacity, width)
    incoming = lax.all_to_all(outgoing, "expert", split_axis=0, concat_axis=0, tiled=True)
    expert_token_rows = incoming.reshape(expert_count * capacity, width)
    expert_gate_portion = matmul(expert_token_rows, expert_gate_activation)
    expert_up_portion = matmul(expert_token_rows, expert_up_projection)
    expert_inner = gated(expert_gate_portion, expert_up_portion).astype(jnp.bfloat16)
    expert_result = (
        matmul(expert_inner, expert_downward)
        .astype(jnp.bfloat16)
        .reshape(expert_count, capacity, width)
    )
    returned = lax.all_to_all(expert_result, "expert", split_axis=0, concat_axis=0, tiled=True)
    picked = returned.reshape(expert_count * capacity, width)[slots].reshape(
        token_count, TOP, width
    )
    picked_float = picked.astype(jnp.float32)
    routed = jnp.einsum("tj,tjd->td", gates, picked_float)
    output = after_attn + routed + shared_result
    grad_top = cotangent.astype(jnp.float32)
    grad_shared_down = multiply_transposed_left(shared_inner, cotangent)
    grad_shared_inner = multiply_transposed_right(cotangent, shared_downward)
    grad_sgate, grad_sup = gated_gradient_rows(shared_gate_part, shared_up_part, grad_shared_inner)
    grad_sgate_low = grad_sgate.astype(jnp.bfloat16)
    grad_sup_low = grad_sup.astype(jnp.bfloat16)
    grad_shared_gate = multiply_transposed_left(normed_second, grad_sgate_low)
    grad_shared_up = multiply_transposed_left(normed_second, grad_sup_low)
    grad_normed = multiply_transposed_right(
        grad_sgate_low, shared_gating
    ) + multiply_transposed_right(grad_sup_low, shared_upward)
    grad_gates = jnp.einsum("td,tjd->tj", grad_top, picked_float)
    grad_chosen = gates * (grad_gates - jnp.sum(gates * grad_gates, axis=-1, keepdims=True))
    route_onehot = (
        routes[:, :, None] == jnp.arange(expert_count, dtype=jnp.int32)[None, None, :]
    ).astype(jnp.float32)
    grad_logits = jnp.einsum("tj,tje->te", grad_chosen, route_onehot).astype(jnp.bfloat16)
    grad_router = multiply_transposed_left(normed_second, grad_logits)
    grad_normed = grad_normed + multiply_transposed_right(grad_logits, router_weight)
    grad_copies = (
        (gates[:, :, None] * grad_top[:, None, :])
        .astype(jnp.bfloat16)
        .reshape(token_count * TOP, width)
    )
    padded_grads = jnp.concatenate([grad_copies, jnp.zeros((1, width), jnp.bfloat16)], axis=0)
    grad_outgoing = padded_grads[owners].reshape(expert_count, capacity, width)
    grad_incoming = lax.all_to_all(
        grad_outgoing, "expert", split_axis=0, concat_axis=0, tiled=True
    ).reshape(expert_count * capacity, width)
    grad_expert_down = multiply_transposed_left(expert_inner, grad_incoming)
    inner_gradient_rows = multiply_transposed_right(grad_incoming, expert_downward)
    gradient_expert_gate_rows, gradient_expert_up_rows = gated_gradient_rows(
        expert_gate_portion, expert_up_portion, inner_gradient_rows
    )
    gradient_expert_gate_reduced = gradient_expert_gate_rows.astype(jnp.bfloat16)
    gradient_expert_up_reduced = gradient_expert_up_rows.astype(jnp.bfloat16)
    grad_expert_gate = multiply_transposed_left(expert_token_rows, gradient_expert_gate_reduced)
    expert_up_weight_gradient = multiply_transposed_left(
        expert_token_rows, gradient_expert_up_reduced
    )
    grad_rows = (
        multiply_transposed_right(gradient_expert_gate_reduced, expert_gate_activation)
        + multiply_transposed_right(gradient_expert_up_reduced, expert_up_projection)
    ).astype(jnp.bfloat16)
    grad_rows = grad_rows.reshape(expert_count, capacity, width)
    grad_returned = lax.all_to_all(grad_rows, "expert", split_axis=0, concat_axis=0, tiled=True)
    grad_picked = grad_returned.reshape(expert_count * capacity, width)[slots].reshape(
        token_count, TOP, width
    )
    grad_normed = grad_normed + jnp.sum(grad_picked.astype(jnp.float32), axis=1)
    gate_share, up_share, down_share = (
        lax.psum_scatter(
            grad_expert_gate[None].astype(jnp.bfloat16), "fsdp", scatter_dimension=1, tiled=True
        ).astype(jnp.float32),
        lax.psum_scatter(
            expert_up_weight_gradient[None].astype(jnp.bfloat16),
            "fsdp",
            scatter_dimension=1,
            tiled=True,
        ).astype(jnp.float32),
        lax.psum_scatter(
            grad_expert_down[None].astype(jnp.bfloat16), "fsdp", scatter_dimension=1, tiled=True
        ).astype(jnp.float32),
    )
    unused, second_pull = jax.vjp(normalize, after_attn, gain_second)
    grad_after, grad_gain_two = second_pull(grad_normed)
    grad_after = grad_after + grad_top
    grad_attn_low = grad_after.astype(jnp.bfloat16)
    grad_output_weight = multiply_transposed_left(mixture, grad_attn_low)
    grad_mixture = (
        multiply_transposed_right(grad_attn_low, output_weight)
        .astype(jnp.bfloat16)
        .reshape(token_count, HEADS, HEAD_DIM)
    )
    grad_query_rot, grad_key_rot, grad_value_float = attend_backward(
        query_states, key_states, value_states, grad_mixture, log_total, block_rows, score_scale
    )
    grad_query_raw = (
        rotate(grad_query_rot, cosine, -sine).astype(jnp.bfloat16).reshape(token_count, width)
    )
    grad_key_raw = (
        rotate(grad_key_rot, cosine, -sine).astype(jnp.bfloat16).reshape(token_count, width)
    )
    grad_value_low = grad_value_float.astype(jnp.bfloat16).reshape(token_count, width)
    grad_query_weight = multiply_transposed_left(normed_first, grad_query_raw)
    grad_key_weight = multiply_transposed_left(normed_first, grad_key_raw)
    grad_value_weight = multiply_transposed_left(normed_first, grad_value_low)
    grad_first = (
        multiply_transposed_right(grad_query_raw, query_weight)
        + multiply_transposed_right(grad_key_raw, key_weight)
        + multiply_transposed_right(grad_value_low, value_weight)
    )
    unused_first, first_pull = jax.vjp(normalize, residual, gain_first)
    grad_residual, grad_gain_one = first_pull(grad_first)
    grad_hidden = grad_residual + grad_after
    summed = (
        lax.psum_scatter(grad_gain_one, ("expert", "fsdp"), scatter_dimension=0, tiled=True),
        lax.psum_scatter(grad_query_weight, ("expert", "fsdp"), scatter_dimension=0, tiled=True),
        lax.psum_scatter(grad_key_weight, ("expert", "fsdp"), scatter_dimension=0, tiled=True),
        lax.psum_scatter(grad_value_weight, ("expert", "fsdp"), scatter_dimension=0, tiled=True),
        lax.psum_scatter(grad_output_weight, ("expert", "fsdp"), scatter_dimension=0, tiled=True),
        lax.psum_scatter(grad_gain_two, ("expert", "fsdp"), scatter_dimension=0, tiled=True),
        lax.psum_scatter(grad_router, ("expert", "fsdp"), scatter_dimension=0, tiled=True),
        lax.psum_scatter(grad_shared_gate, ("expert", "fsdp"), scatter_dimension=0, tiled=True),
        lax.psum_scatter(grad_shared_up, ("expert", "fsdp"), scatter_dimension=0, tiled=True),
        lax.psum_scatter(grad_shared_down, ("expert", "fsdp"), scatter_dimension=0, tiled=True),
    )
    return (
        output.astype(jnp.bfloat16),
        grad_hidden,
        summed[0],
        summed[1],
        summed[2],
        summed[3],
        summed[4],
        summed[5],
        summed[6],
        summed[7],
        summed[8],
        summed[9],
        gate_share,
        up_share,
        down_share,
    )


def solution(mesh):
    return jax.shard_map(
        per_device,
        mesh=mesh,
        in_specs=(
            P(("expert", "fsdp"), None),
            P(("expert", "fsdp"), None),
            P(("expert", "fsdp")),
            P(("expert", "fsdp"), None),
            P(("expert", "fsdp"), None),
            P(("expert", "fsdp"), None),
            P(("expert", "fsdp"), None),
            P(("expert", "fsdp")),
            P(("expert", "fsdp"), None),
            P(("expert", "fsdp"), None),
            P(("expert", "fsdp"), None),
            P(("expert", "fsdp"), None),
            P("expert", "fsdp", None),
            P("expert", "fsdp", None),
            P("expert", "fsdp", None),
            P(("expert", "fsdp"), None),
        ),
        out_specs=(
            P(("expert", "fsdp"), None),
            P(("expert", "fsdp"), None),
            P(("expert", "fsdp")),
            P(("expert", "fsdp"), None),
            P(("expert", "fsdp"), None),
            P(("expert", "fsdp"), None),
            P(("expert", "fsdp"), None),
            P(("expert", "fsdp")),
            P(("expert", "fsdp"), None),
            P(("expert", "fsdp"), None),
            P(("expert", "fsdp"), None),
            P(("expert", "fsdp"), None),
            P("expert", "fsdp", None),
            P("expert", "fsdp", None),
            P("expert", "fsdp", None),
        ),
        check_vma=False,
    )
```

profile of v0, /device:TPU:0, one launch (start us, length us, event | category | flops | bytes accessed | tf_op | source)
XLA Modules:
  0.0 1582.7 jit_solution(14775567727401140315)
XLA Ops:
  14.7 42.1 %all-reduce.8 = (bf16[768]{0:T(1024)(128)(2,1)S(1)}, bf16[768]{0:T(1024)(128)(2,1)S(1)}) all-reduce(bf16[768]{0:T(1024)(128)(2,1)S(1)} %dynamic-update-slice, bf16[768]{0:T(1024)(128)(2,1)S(1)} %dynamic-update-slice.1), channel_id=1, replica_groups=mesh['expert'=8,'fsdp'=4] {'expert','fsdp'}, use_global_device_ids=true, to_apply=%add.2 | all-reduce | flops 1536 | bytes 6144
  62.6 4.5 scatter_custom_fusion
  69.9 53.7 %all-gather.16.cloned.1.call-done = bf16[768,768]{1,0:T(8,128)(2,1)} async-done(((bf16[24,768]{1,0:T(8,128)(2,1)}), bf16[768,768]{1,0:T(8,128)(2,1)}) %all-gather.16.cloned.1.call-update) | async-done | bytes 1179664 | tf_op jit(solution)/shard_map/all_gather | solution.py:173
  127.5 5.8 fusion.10
  133.3 46.1 %all-gather.12.cloned.1.call-done = bf16[768,768]{1,0:T(8,128)(2,1)} async-done(((bf16[24,768]{1,0:T(8,128)(2,1)}), bf16[768,768]{1,0:T(8,128)(2,1)}) %all-gather.12.cloned.1.call-update) | async-done | bytes 1179664 | tf_op jit(solution)/shard_map/all_gather | solution.py:174
  181.8 7.5 fusion.4
  190.3 3.6 fusion.46
  193.9 41.2 %all-gather.18.cloned.1.call-done = bf16[768,768]{1,0:T(8,128)(2,1)} async-done(((bf16[24,768]{1,0:T(8,128)(2,1)}), bf16[768,768]{1,0:T(8,128)(2,1)}) %all-gather.18.cloned.1.call-update) | async-done | bytes 1179664 | tf_op jit(solution)/shard_map/all_gather | solution.py:175
  238.7 9.4 gather_fusion
  248.1 3.6 all-to-all-start
  253.3 26.3 %all-gather.20.cloned.1.call-done = bf16[1,768,2048]{2,1,0:T(8,128)(2,1)} async-done(((bf16[1,192,2048]{2,1,0:T(8,128)(2,1)}), bf16[1,768,2048]{2,1,0:T(8,128)(2,1)}) %all-gather.20.cloned.1.call-update) | async-done | bytes 3145744 | tf_op jit(solution)/shard_map/all_gather | solution.py:195
  279.5 43.7 %all-to-all-done = bf16[8,256,768]{2,1,0:T(8,128)(2,1)S(1)} async-done(((bf16[8,256,768]{2,1,0:T(8,128)(2,1)}), bf16[8,256,768]{2,1,0:T(8,128)(2,1)S(1)}, u32[]{:S(2)}, u32[]{:S(2)}) %all-to-all-start) | async-done | bytes 3145760 | tf_op jit(solution)/shard_map/all_to_all | solution.py:237
  323.2 12.6 fusion.24
  335.8 16.8 %multiply_convert_fusion.1 = (bf16[2048,2048]{1,0:T(8,128)(2,1)}, f32[2048,2048]{1,0:T(8,128)}) fusion(f32[2048,2048]{1,0:T(8,128)} %fusion.24, bf16[2048,768]{1,0:T(8,128)(2,1)S(1)} %bitcast.174, bf16[1,768,2048]{2,1,0:T(8,128)(2,1)} %all-gather.22.cloned.1.call-done), kind=kOutput, calls=%fused_computation.11 | convolution fusion | flops 6467616768 | bytes 48234496 | tf_op jit(solution)/shard_map/dot_general | solution.py:34
  352.6 18.2 %all-gather.24.cloned.1.call-done = bf16[1,2048,768]{2,1,0:T(8,128)(2,1)} async-done(((bf16[1,512,768]{2,1,0:T(8,128)(2,1)}), bf16[1,2048,768]{2,1,0:T(8,128)(2,1)}) %all-gather.24.cloned.1.call-update) | async-done | bytes 3145744 | tf_op jit(solution)/shard_map/all_gather | solution.py:197
  370.8 11.2 convolution_convert_fusion.2
  382.0 4.7 all-to-all-start.1
  387.5 126.1 %all-gather = bf16[32,24,8]{1,2,0:T(8,128)(2,1)S(1)} all-gather(bf16[1,24,8]{1,2,0:T(8,128)(2,1)S(1)} %bitcast.198), channel_id=1, replica_groups=mesh['expert'=8,'fsdp'=4] {'expert','fsdp'}, dimensions={0}, use_global_device_ids=true | all-gather | bytes 12672 | tf_op jit(solution)/shard_map/all_gather | solution.py:177
  514.1 3.7 mul.529
  517.8 5.2 mul.530
  524.5 6.5 gather_fusion.4
  531.5 5.2 gather_fusion.1
  536.7 4.5 reshape.344
  541.2 4.8 fusion.41
  547.8 9.4 gather_fusion.2
  557.2 7.2 all-to-all-start.2
  565.1 85.4 %all-to-all-done.2 = bf16[8,256,768]{2,1,0:T(8,128)(2,1)S(1)} async-done(((bf16[8,256,768]{2,1,0:T(8,128)(2,1)}), bf16[8,256,768]{2,1,0:T(8,128)(2,1)S(1)}, u32[]{:S(2)}, u32[]{:S(2)}) %all-to-all-start.2) | async-done | bytes 3145760 | tf_op jit(solution)/shard_map/all_to_all | solution.py:280
  650.6 11.5 fusion.26
  662.2 25.6 %fusion.2 = (bf16[2048,2048]{1,0:T(8,128)(2,1)}, bf16[2048,2048]{1,0:T(8,128)(2,1)}) fusion(f32[2048,2048]{1,0:T(8,128)} %fusion.24, f32[2048,2048]{1,0:T(8,128)} %get-tuple-element.100, bf16[2048,768]{1,0:T(8,128)(2,1)} %bitcast.180, bf16[1,2048,768]{2,1,0:T(8,128)(2,1)} %all-gather.24.cloned.1.call-done), kind=kOutput, calls=%fused_computation.9 | convolution fusion | flops 6501171200 | bytes 56623104 | tf_op jit(solution)/shard_map/dot_general | solution.py:44
  687.8 10.3 fusion.27
  698.4 10.4 fusion.28
  710.0 5.7 fusion.104
  715.7 5.8 fusion.105
  721.5 7.8 multiply_convert_fusion.3
  730.7 4.4 fusion.110
  736.7 4.5 fusion.111
  743.1 9.3 fusion.18
  752.5 10.3 add_convert_fusion
  762.8 3.7 all-to-all-start.3
  766.5 6.5 fusion.112
  773.8 5.7 fusion.106
  779.5 3.1 fusion.107
  783.5 2.5 fusion.47
  786.1 51.8 %all-to-all-done.3 = bf16[8,256,768]{2,1,0:T(8,128)(2,1)S(1)} async-done(((bf16[8,256,768]{2,1,0:T(8,128)(2,1)}), bf16[8,256,768]{2,1,0:T(8,128)(2,1)S(1)}, u32[]{:S(2)}, u32[]{:S(2)}) %all-to-all-start.3) | async-done | bytes 3145760 | tf_op jit(solution)/shard_map/all_to_all | solution.py:299
  837.9 5.4 gather_fusion.3
  843.2 4.9 reshape.351
  848.2 5.7 reduce_sum.127
  854.0 2.7 multiply_reduce_fusion.1
  861.5 11.1 multiply_reduce_fusion
  874.2 7.3 multiply_convert_fusion.2
  889.7 3.6 fusion.91
  893.4 3.9 fusion.51
  897.3 6.4 fusion.43
  908.2 3.5 fusion.103
  911.8 2.7 fusion.40
  918.8 37.4 %all-reduce.7 = (f32[768]{0:T(1024)S(1)}, f32[768]{0:T(1024)S(1)}, f32[768,8]{0,1:T(8,128)S(1)}) all-reduce(f32[768]{0:T(1024)S(1)} %get-tuple-element.62, f32[768]{0:T(1024)S(1)} %get-tuple-element.60, f32[768,8]{0,1:T(8,128)S(1)} %fusion.55), channel_id=2, replica_groups=mesh['expert'=8,'fsdp'=4] {'expert','fsdp'}, use_global_device_ids=true, to_apply=%region_16.17.clone | all-reduce | flops 7680 | bytes 61440
  958.0 3.0 fusion.36
  963.5 2.5 convert_element_type.175
  968.4 69.7 %reduce-scatter.22.cloned.1.call-done = f32[24,2048]{1,0:T(8,128)} async-done(((f32[768,2048]{1,0:T(8,128)}), f32[24,2048]{1,0:T(8,128)}) %reduce-scatter.22.cloned.1.call-update) | async-done | bytes 196624 | tf_op jit(solution)/shard_map/reduce_scatter | solution.py:358
  1038.1 120.0 %reduce-scatter.24.cloned.1.call-done = f32[64,768]{1,0:T(8,128)} async-done(((f32[2048,768]{1,0:T(8,128)}), f32[64,768]{1,0:T(8,128)}) %reduce-scatter.24.cloned.1.call-update) | async-done | bytes 196624 | tf_op jit(solution)/shard_map/reduce_scatter | solution.py:359
  1158.1 104.3 %reduce-scatter.12.cloned.1.call-done = f32[24,768]{1,0:T(8,128)} async-done(((f32[768,768]{1,0:T(8,128)}), f32[24,768]{1,0:T(8,128)}) %reduce-scatter.12.cloned.1.call-update) | async-done | bytes 73744 | tf_op jit(solution)/shard_map/reduce_scatter | solution.py:351
  1262.4 104.4 %reduce-scatter.14.cloned.1.call-done = f32[24,768]{1,0:T(8,128)} async-done(((f32[768,768]{1,0:T(8,128)}), f32[24,768]{1,0:T(8,128)}) %reduce-scatter.14.cloned.1.call-update) | async-done | bytes 73744 | tf_op jit(solution)/shard_map/reduce_scatter | solution.py:352
  1366.8 104.5 %reduce-scatter.18.cloned.1.call-done = f32[24,768]{1,0:T(8,128)} async-done(((f32[768,768]{1,0:T(8,128)}), f32[24,768]{1,0:T(8,128)}) %reduce-scatter.18.cloned.1.call-update) | async-done | bytes 73744 | tf_op jit(solution)/shard_map/reduce_scatter | solution.py:354
  1471.4 104.2 %reduce-scatter.16.cloned.1.call-done = f32[24,768]{1,0:T(8,128)} async-done(((f32[768,768]{1,0:T(8,128)}), f32[24,768]{1,0:T(8,128)}) %reduce-scatter.16.cloned.1.call-update) | async-done | bytes 73744 | tf_op jit(solution)/shard_map/reduce_scatter | solution.py:353
  (296 shorter events, 71.8 us)
Async XLA Ops:
  7.2 60.6 %copy-start.4 = (bf16[512,768]{1,0:T(8,128)(2,1)S(1)}, bf16[512,768]{1,0:T(8,128)(2,1)}, u32[]{:S(2)}) copy-start(bf16[512,768]{1,0:T(8,128)(2,1)} %param.16) | copy-start | bytes 2359300
  7.2 60.5 %all-gather.14.cloned.1.call-start = ((), (), s32[]{:S(2)}) async-start(), calls=%async_computation.15 | async-start | bytes 1216512 | tf_op jit(solution)/shard_map/all_gather | solution.py:172
  7.9 115.7 %all-gather.16.cloned.1.call-start = ((), (), s32[]{:S(2)}) async-start(), calls=%async_computation.16 | async-start | bytes 1216512 | tf_op jit(solution)/shard_map/all_gather | solution.py:173
  8.7 170.7 %all-gather.12.cloned.1.call-start = ((), (), s32[]{:S(2)}) async-start(), calls=%async_computation.14 | async-start | bytes 1216512 | tf_op jit(solution)/shard_map/all_gather | solution.py:174
  9.4 225.7 %all-gather.18.cloned.1.call-start = ((), (), s32[]{:S(2)}) async-start(), calls=%async_computation.17 | async-start | bytes 1216512 | tf_op jit(solution)/shard_map/all_gather | solution.py:175
  10.0 269.5 %all-gather.20.cloned.1.call-start = ((), (), s32[]{:S(2)}) async-start(), calls=%async_computation.18 | async-start | bytes 3932160 | tf_op jit(solution)/shard_map/all_gather | solution.py:195
  10.6 325.2 %all-gather.22.cloned.1.call-start = ((), (), s32[]{:S(2)}) async-start(), calls=%async_computation.19 | async-start | bytes 3932160 | tf_op jit(solution)/shard_map/all_gather | solution.py:196
  12.0 46.2 %copy-start.26 = (s32[512,2]{1,0:T(8,128)}, s32[512,2]{1,0:T(8,128)S(1)}, u32[]{:S(2)}) copy-start(s32[512,2]{1,0:T(8,128)S(1)} %copy.88) | copy-start | bytes 12292
  56.8 122.6 %copy-start.46 = (f32[768]{0:T(1024)}, f32[768]{0:T(1024)S(1)}, u32[]{:S(2)}) copy-start(f32[768]{0:T(1024)S(1)} %convert_element_type.141) | copy-start | bytes 9220
  58.2 121.2 %copy-start.54 = (f32[512]{0:T(512)}, f32[512]{0:T(512)S(1)}, u32[]{:S(2)}) copy-start(f32[512]{0:T(512)S(1)} %fusion.80) | copy-start | bytes 6148
  59.2 66.7 %copy-start.43 = (f32[512,32]{0,1:T(8,128)}, f32[512,32]{0,1:T(8,128)S(1)}, u32[]{:S(2)}) copy-start(f32[512,32]{0,1:T(8,128)S(1)} %get-tuple-element.94) | copy-start | bytes 196612
  59.4 129.9 %copy-start.13 = (pred[512,512]{0,1:T(8,128)(4,1)}, pred[512,512]{0,1:T(8,128)(4,1)S(1)}, u32[]{:S(2)}) copy-start(pred[512,512]{0,1:T(8,128)(4,1)S(1)} %broadcast_compare_fusion) | copy-start | bytes 786436
  59.4 177.9 %copy-start.59 = (f32[768]{0:T(1024)}, f32[768]{0:T(1024)S(1)}, u32[]{:S(2)}) copy-start(f32[768]{0:T(1024)S(1)} %convert_element_type.147) | copy-start | bytes 9220
  133.3 56.0 %copy-start.48 = (f32[12,512]{1,0:T(8,128)}, f32[12,512]{1,0:T(8,128)S(1)}, u32[]{:S(2)}) copy-start(f32[12,512]{1,0:T(8,128)S(1)} %get-tuple-element.95) | copy-start | bytes 73732
  181.8 7.5 copy-start.15
  181.8 8.5 copy-start
  193.9 43.6 %copy-start.42 = (bf16[12,64,512]{2,1,0:T(8,128)(2,1)}, bf16[12,64,512]{2,1,0:T(8,128)(2,1)S(1)}, u32[]{:S(2)}) copy-start(bf16[12,64,512]{2,1,0:T(8,128)(2,1)S(1)} %fusion.46) | copy-start | bytes 2359300
  237.3 10.8 copy-start.70
  237.3 10.8 copy-start.65
  248.1 75.1 %all-to-all-start = ((bf16[8,256,768]{2,1,0:T(8,128)(2,1)}), bf16[8,256,768]{2,1,0:T(8,128)(2,1)S(1)}, u32[]{:S(2)}, u32[]{:S(2)}) async-start(bf16[8,256,768]{2,1,0:T(8,128)(2,1)} %bitcast.166), calls=%async_computation | async-start | bytes 6291456 | tf_op jit(solution)/shard_map/all_to_all | solution.py:237
  251.7 119.1 %all-gather.24.cloned.1.call-start = ((), (), s32[]{:S(2)}) async-start(), calls=%async_computation.20 | async-start | bytes 3932160 | tf_op jit(solution)/shard_map/all_gather | solution.py:197
  252.5 456.5 %all-gather.26.cloned.1.call-start = ((), (), s32[]{:S(2)}) async-start(), calls=%async_computation.21 | async-start | bytes 3244032 | tf_op jit(solution)/shard_map/all_gather | solution.py:178
  323.2 12.6 copy-start.17
  382.0 5.5 copy-start.73
  382.0 131.8 %copy-start.58 = (s32[512,2]{0,1:T(2,128)S(1)}, s32[512,2]{0,1:T(2,128)}, u32[]{:S(2)}) copy-start(s32[512,2]{0,1:T(2,128)} %param.17) | copy-start | bytes 12292
  382.0 149.5 %all-to-all-start.1 = ((bf16[8,256,768]{2,1,0:T(8,128)(2,1)}), bf16[8,256,768]{2,1,0:T(8,128)(2,1)S(1)}, u32[]{:S(2)}, u32[]{:S(2)}) async-start(bf16[8,256,768]{2,1,0:T(8,128)(2,1)} %bitcast.177), calls=%async_computation.1 | async-start | bytes 6291456 | tf_op jit(solution)/shard_map/all_to_all | solution.py:247
  386.7 328.9 %all-gather.28.cloned.1.call-start = ((), (), s32[]{:S(2)}) async-start(), calls=%async_computation.22 | async-start | bytes 3244032 | tf_op jit(solution)/shard_map/all_gather | solution.py:179
  513.8 9.3 copy-start.52
  523.1 8.4 copy-start.63
  541.2 5.9 copy-start.10
  557.2 93.4 %all-to-all-start.2 = ((bf16[8,256,768]{2,1,0:T(8,128)(2,1)}), bf16[8,256,768]{2,1,0:T(8,128)(2,1)S(1)}, u32[]{:S(2)}, u32[]{:S(2)}) async-start(bf16[8,256,768]{2,1,0:T(8,128)(2,1)} %bitcast.167), calls=%async_computation.2 | async-start | bytes 6291456 | tf_op jit(solution)/shard_map/all_to_all | solution.py:280
  564.3 157.1 %all-gather.30.cloned.1.call-start = ((), (), s32[]{:S(2)}) async-start(), calls=%async_computation.23 | async-start | bytes 3244032 | tf_op jit(solution)/shard_map/all_gather | solution.py:180
  564.9 396.1 %reduce-scatter.30.cloned.1.call-start = ((), (), s32[]{:S(2)}) async-start(), calls=%async_computation.33 | async-start | bytes 3932160 | tf_op jit(solution)/shard_map/reduce_scatter | solution.py:314
  650.6 11.5 copy-start.19
  662.1 301.3 %reduce-scatter.26.cloned.1.call-start = ((), (), s32[]{:S(2)}) async-start(), calls=%async_computation.31 | async-start | bytes 3932160 | tf_op jit(solution)/shard_map/reduce_scatter | solution.py:305
  662.2 25.6 %copy-start.18 = (bf16[8,256,768]{2,1,0:T(8,128)(2,1)S(1)}, bf16[8,256,768]{2,1,0:T(8,128)(2,1)}, u32[]{:S(2)}) copy-start(bf16[8,256,768]{2,1,0:T(8,128)(2,1)} %copy-done.17) | copy-start | bytes 9437188
  698.2 267.8 %reduce-scatter.28.cloned.1.call-start = ((), (), s32[]{:S(2)}) async-start(), calls=%async_computation.32 | async-start | bytes 3932160 | tf_op jit(solution)/shard_map/reduce_scatter | solution.py:308
  708.9 259.5 %reduce-scatter.20.cloned.1.call-start = ((), (), s32[]{:S(2)}) async-start(), calls=%async_computation.28 | async-start | bytes 6488064 | tf_op jit(solution)/shard_map/reduce_scatter | solution.py:357
  715.7 5.8 copy-start.11
  735.2 302.9 %reduce-scatter.22.cloned.1.call-start = ((), (), s32[]{:S(2)}) async-start(), calls=%async_computation.29 | async-start | bytes 6488064 | tf_op jit(solution)/shard_map/reduce_scatter | solution.py:358
  743.1 9.3 copy-start.74
  762.8 75.1 %all-to-all-start.3 = ((bf16[8,256,768]{2,1,0:T(8,128)(2,1)}), bf16[8,256,768]{2,1,0:T(8,128)(2,1)S(1)}, u32[]{:S(2)}, u32[]{:S(2)}) async-start(bf16[8,256,768]{2,1,0:T(8,128)(2,1)} %bitcast.178), calls=%async_computation.3 | async-start | bytes 6291456 | tf_op jit(solution)/shard_map/all_to_all | solution.py:299
  766.4 391.7 %reduce-scatter.24.cloned.1.call-start = ((), (), s32[]{:S(2)}) async-start(), calls=%async_computation.30 | async-start | bytes 6488064 | tf_op jit(solution)/shard_map/reduce_scatter | solution.py:359
  773.0 489.4 %reduce-scatter.12.cloned.1.call-start = ((), (), s32[]{:S(2)}) async-start(), calls=%async_computation.24 | async-start | bytes 2433024 | tf_op jit(solution)/shard_map/reduce_scatter | solution.py:351
  773.8 5.7 copy-start.29
  773.8 5.7 copy-start.77
  779.5 4.0 copy-start.27
  782.6 55.3 %copy-start.64 = (s32[1024]{0:T(1024)S(1)}, s32[1024]{0:T(1024)}, u32[]{:S(2)}) copy-start(s32[1024]{0:T(1024)} %copy-done.63) | copy-start | bytes 12292
  848.1 5.8 copy-start.7
  848.1 5.8 copy-start.40
  848.1 5.8 copy-start.53
  848.1 5.8 copy-start.60
  848.1 5.8 copy-start.66
  861.4 11.1 slice-start
  861.4 11.1 slice-start.1
  861.4 12.8 slice-start.2
  874.2 7.3 copy-start.36
  874.2 7.3 copy-start.38
  889.7 477.1 %reduce-scatter.14.cloned.1.call-start = ((), (), s32[]{:S(2)}) async-start(), calls=%async_computation.25 | async-start | bytes 2433024 | tf_op jit(solution)/shard_map/reduce_scatter | solution.py:352
  893.3 578.1 %reduce-scatter.18.cloned.1.call-start = ((), (), s32[]{:S(2)}) async-start(), calls=%async_computation.27 | async-start | bytes 2433024 | tf_op jit(solution)/shard_map/reduce_scatter | solution.py:354
  897.3 678.3 %reduce-scatter.16.cloned.1.call-start = ((), (), s32[]{:S(2)}) async-start(), calls=%async_computation.26 | async-start | bytes 2433024 | tf_op jit(solution)/shard_map/reduce_scatter | solution.py:353
  911.7 3.5 copy-start.78
  916.4 41.6 %copy-start.69 = (f32[512]{0:T(512)S(1)}, f32[512]{0:T(512)}, u32[]{:S(2)}) copy-start(f32[512]{0:T(512)} %copy-done.68) | copy-start | bytes 6148
  916.4 41.6 %copy-start.9 = (f32[512,768]{1,0:T(8,128)S(1)}, f32[512,768]{1,0:T(8,128)}, u32[]{:S(2)}) copy-start(f32[512,768]{1,0:T(8,128)} %copy-done.8) | copy-start | bytes 4718596
  (44 other events, 81.9 us)
Sparse Core Ops, SparseCore 0:
  10.9 56.7 all-gather.13
  70.6 52.9 all-gather.15
  126.5 52.8 all-gather.11
  182.2 52.8 all-gather.17
  236.8 42.7 all-gather.19
  281.2 43.8 all-gather.21
  326.9 43.8 all-gather.23
  373.7 87.6 all-gather.25
  464.3 58.1 all-gather.27
  567.7 72.8 all-gather.29
  662.3 40.9 reduce-scatter.29
  706.1 43.8 reduce-scatter.25
  753.0 43.8 reduce-scatter.27
  803.0 114.9 reduce-scatter.19
  924.1 113.9 reduce-scatter.21
  1044.1 113.9 reduce-scatter.23
  1163.8 98.5 reduce-scatter.11
  1268.1 98.6 reduce-scatter.13
  1372.7 98.6 reduce-scatter.17
  1477.1 98.4 reduce-scatter.15
where the time goes:
time: 1590 us; the launch traced here: 1580 us
  waiting for transfers between devices  980 us (62%)
  matrix products  236 us (15%)
  blocking collectives  206 us (13%)
  local copies, waits for them, and re-layouts  83.8 us (5%)
  other arithmetic  40.9 us (3%)
  starting transfers between devices  21 us (1%)
    all_gather x1, blocking collectives, per_device(): lax.all_gather(w_router, ('expert', 'fsdp'), axis=0, tiled=True)  126 us
    reduce_scatter x1, waiting for transfers between devices, per_device(): lax.psum_scatter(grad_shared_down, ('expert', 'fsdp'), scatter_dimension=...  120 us
    reduce_scatter x1, waiting for transfers between devices, per_device(): lax.psum_scatter(grad_output_weight, ('expert', 'fsdp'), scatter_dimensio...  105 us
    reduce_scatter x1, waiting for transfers between devices, per_device(): lax.psum_scatter(grad_key_weight, ('expert', 'fsdp'), scatter_dimension=0...  104 us
    reduce_scatter x1, waiting for transfers between devices, per_device(): lax.psum_scatter(grad_query_weight, ('expert', 'fsdp'), scatter_dimension...  104 us
    reduce_scatter x1, waiting for transfers between devices, per_device(): lax.psum_scatter(grad_value_weight, ('expert', 'fsdp'), scatter_dimension...  104 us
    all_to_all x1, waiting for transfers between devices, per_device(): lax.all_to_all(grad_outgoing, 'expert', split_axis=0, concat_axis=0, tile...  85.4 us
    unnamed x2, blocking collectives  79.5 us
  transfers between devices with their start and end apart: 24, of which 14 were waited for; matrix products, arithmetic and copies ran while one was open for 22% of the time, Pallas kernels for 0%

commit v1 on v0

v1 whole, which is shorter than its diff:
```python
import functools

import jax
import jax.numpy as jnp
from jax import lax
from jax.sharding import PartitionSpec as P

HEADS = 12
HEAD_DIM = 64
BLOCK = 256
CHUNK = 256
ALL = ("expert", "fsdp")
EPSILON = 1e-06
BF = jnp.bfloat16
F32 = jnp.float32


def rope_tables(length, head_size):
    half = head_size // 2
    freqs = jnp.exp(-jnp.log(10000.0) * jnp.arange(half, dtype=F32) * 2.0 / head_size)
    angles = jnp.arange(length, dtype=F32)[:, None] * freqs[None, :]
    return (jnp.cos(angles)[:, None, :], jnp.sin(angles)[:, None, :])


def rotate(values, cosine, sine):
    half = values.shape[-1] // 2
    first = values[..., :half]
    second = values[..., half:]
    return jnp.concatenate(
        [first * cosine - second * sine, second * cosine + first * sine], axis=-1
    )


def dot(left, right, contract):
    return lax.dot_general(left, right, (contract, ((), ())), preferred_element_type=F32)


def mm(left, right):
    return dot(left, right, ((1,), (0,)))


def mm_tl(left, right):
    return dot(left, right, ((0,), (0,)))


def mm_tr(left, right):
    return dot(left, right, ((1,), (1,)))


def gated_backward(gate_part, up_part, grad):
    sig = jax.nn.sigmoid(gate_part)
    silu = gate_part * sig
    grad_gate = (grad * up_part * (sig * (1.0 + gate_part * (1.0 - sig)))).astype(BF)
    grad_up = (grad * silu).astype(BF)
    return grad_gate, grad_up


def norm_backward(values, scale, gain, grad):
    weighted = gain * grad
    inner = jnp.mean(weighted * values, axis=-1, keepdims=True)
    grad_values = scale * weighted - values * (scale * scale * scale) * inner
    return grad_values, jnp.sum(grad * values * scale, axis=0)


def to_chunks(block):
    rows, columns = block.shape
    return block.reshape(rows, columns // CHUNK, CHUNK).transpose(1, 0, 2).reshape(-1, CHUNK)


def from_chunks(gathered, rows, columns):
    parts = gathered.shape[0]
    return (
        gathered.reshape(parts, columns // CHUNK, rows, CHUNK)
        .transpose(0, 2, 1, 3)
        .reshape(parts * rows, columns)
    )


def split_chunks(full, parts):
    rows = full.shape[0] // parts
    columns = full.shape[1]
    return (
        full.reshape(parts, rows, columns // CHUNK, CHUNK)
        .transpose(0, 2, 1, 3)
        .reshape(parts, rows * columns // CHUNK, CHUNK)
    )


def gather_fsdp(block, n_f):
    if n_f != 4:
        return lax.all_gather(block, "fsdp", axis=0, tiled=True)
    rows = block.shape[0]
    own = lax.axis_index("fsdp")
    full = jnp.zeros((n_f * rows,) + block.shape[1:], block.dtype)
    full = lax.dynamic_update_slice(full, block, (own * rows, 0))
    for k in range(1, n_f):
        part = lax.ppermute(block, "fsdp", [(i, i ^ k) for i in range(n_f)])
        full = lax.dynamic_update_slice(full, part, ((own ^ k) * rows, 0))
    return full


def gather_expert(block, n_e):
    index = lax.axis_index("expert")
    height, core = index // 2, index % 2
    levels = n_e // 2
    line = jnp.zeros((levels,) + block.shape, block.dtype)
    line = lax.dynamic_update_slice(line, block[None], (height, 0, 0))
    for k in range(1, levels):
        part = lax.ppermute(block, "expert", [(i, i ^ (2 * k)) for i in range(n_e)])
        line = lax.dynamic_update_slice(line, part[None], (height ^ k, 0, 0))
    other = lax.ppermute(line, "expert", [(i, i ^ 1) for i in range(n_e)])
    full = jnp.zeros((levels, 2) + block.shape, block.dtype)
    full = lax.dynamic_update_slice(full, line[:, None], (0, core, 0, 0))
    full = lax.dynamic_update_slice(full, other[:, None], (0, 1 - core, 0, 0))
    return full.reshape((n_e,) + block.shape)


def attention_forward(query, key, value):
    length = query.shape[0]
    mixes, probs = [], []
    for start in range(0, length, BLOCK):
        stop = start + BLOCK
        scores = jnp.einsum(
            "qhd,khd->hqk", query[start:stop], key[:stop], preferred_element_type=F32
        ) * (HEAD_DIM**-0.5)
        exponent = jnp.exp(scores - jnp.max(scores, axis=-1, keepdims=True))
        prob = exponent / jnp.sum(exponent, axis=-1, keepdims=True)
        mix = jnp.einsum(
            "hqk,khd->qhd", prob.astype(BF), value[:stop], preferred_element_type=F32
        )
        mixes.append(mix.astype(BF).reshape(BLOCK, HEADS * HEAD_DIM))
        probs.append(prob)
    return jnp.concatenate(mixes, axis=0), probs


def attention_backward(query, key, value, grad_mix, probs):
    length = query.shape[0]
    scale = HEAD_DIM**-0.5
    grad_key = jnp.zeros(key.shape, F32)
    grad_value = jnp.zeros(value.shape, F32)
    grad_queries = []
    for index, start in enumerate(range(0, length, BLOCK)):
        stop = start + BLOCK
        prob = probs[index]
        grad_block = grad_mix[start:stop]
        grad_prob = jnp.einsum(
            "qhd,khd->hqk", grad_block, value[:stop], preferred_element_type=F32
        )
        grad_scores = (
            prob * (grad_prob - jnp.sum(prob * grad_prob, axis=-1, keepdims=True))
        ).astype(BF)
        grad_queries.append(
            jnp.einsum("hqk,khd->qhd", grad_scores, key[:stop], preferred_element_type=F32) * scale
        )
        dk = jnp.einsum(
            "hqk,qhd->khd", grad_scores, query[start:stop], preferred_element_type=F32
        )
        dv = jnp.einsum(
            "hqk,qhd->khd", prob.astype(BF), grad_block, preferred_element_type=F32
        )
        pad = ((0, length - stop), (0, 0), (0, 0))
        grad_key = grad_key + jnp.pad(dk * scale, pad)
        grad_value = grad_value + jnp.pad(dv, pad)
    return jnp.concatenate(grad_queries, axis=0), grad_key, grad_value


def per_device(
    hidden_in,
    routes,
    attn_gain,
    w_query,
    w_key,
    w_value,
    w_output,
    ffn_gain,
    w_router,
    shared_gate,
    shared_up,
    shared_down,
    expert_gate,
    expert_up,
    expert_down,
    cotangent,
    n_e,
    n_f,
):
    n_all = n_e * n_f
    tokens, width = hidden_in.shape
    rows = w_query.shape[0]
    n_experts = w_router.shape[1]
    hidden = shared_gate.shape[1]
    down_rows = shared_down.shape[0]
    capacity = 2 * 2 * tokens // n_experts

    extras = jnp.concatenate([attn_gain, ffn_gain, w_router.reshape(-1)])
    extras = jnp.pad(extras, (0, 8 * width - extras.shape[0])).reshape(8, width)
    first = lax.all_gather(
        jnp.concatenate([w_query, w_key, w_value, w_output, extras], axis=0), ALL, axis=0
    )
    w_q, w_k, w_v, w_o = (
        first[:, i * rows : (i + 1) * rows].reshape(n_all * rows, width) for i in range(4)
    )
    tail = first[:, 4 * rows]
    gain_one = tail[:, :rows].reshape(-1).astype(F32)
    gain_two = tail[:, rows : 2 * rows].reshape(-1).astype(F32)
    router = tail[:, 2 * rows : (2 + n_experts) * rows].reshape(n_all * rows, n_experts)

    second = lax.all_gather(
        jnp.concatenate([to_chunks(shared_gate), to_chunks(shared_up), to_chunks(shared_down)]),
        ALL,
        axis=0,
    )
    per = rows * hidden // CHUNK
    s_gate = from_chunks(second[:, :per], rows, hidden)
    s_up = from_chunks(second[:, per : 2 * per], rows, hidden)
    s_down = from_chunks(second[:, 2 * per :], down_rows, width)

    route_rows = jnp.pad(routes.T.astype(BF), ((0, 14), (0, width - tokens)))
    cot_all = gather_expert(jnp.concatenate([cotangent, route_rows], axis=0), n_e)
    e_gate = gather_fsdp(expert_gate[0], n_f)
    e_up = gather_fsdp(expert_up[0], n_f)
    e_down = gather_fsdp(expert_down[0], n_f)

    cosine, sine = rope_tables(tokens, HEAD_DIM)
    x = hidden_in.astype(F32)
    r1 = lax.rsqrt(jnp.mean(x * x, axis=-1, keepdims=True) + EPSILON)
    n1 = (x * r1 * gain_one).astype(BF)
    heads = (tokens, HEADS, HEAD_DIM)
    query = rotate(mm(n1, w_q).reshape(heads), cosine, sine).astype(BF)
    key = rotate(mm(n1, w_k).reshape(heads), cosine, sine).astype(BF)
    value = mm(n1, w_v).astype(BF).reshape(heads)
    mix, probs = attention_forward(query, key, value)
    h = x + mm(mix, w_o)
    r2 = lax.rsqrt(jnp.mean(h * h, axis=-1, keepdims=True) + EPSILON)
    n2 = (h * r2 * gain_two).astype(BF)

    n2_all = lax.all_gather(n2, "expert", axis=0)
    me = lax.axis_index("expert")
    routes_all = cot_all[:, tokens : tokens + 2, :tokens].astype(F32)
    mine = routes_all == me.astype(F32)
    mask = jnp.any(mine, axis=1)
    position = jnp.arange(tokens, dtype=jnp.int32)
    before = (position[:, None] < position[None, :]).astype(BF)
    rank = mm(mask.astype(BF), before)
    slot = jnp.arange(capacity, dtype=F32)
    pick = (mask[:, None, :] & (rank[:, None, :] == slot[None, :, None])).astype(BF)
    other = jnp.sum(routes_all, axis=1) - me.astype(F32)
    other_slot = jnp.einsum("skt,st->sk", pick, other.astype(BF), preferred_element_type=F32)

    def take(source):
        return (
            jnp.einsum("skt,std->skd", pick, source, preferred_element_type=F32)
            .astype(BF)
            .reshape(n_e * capacity, width)
        )

    def put(slots):
        return jnp.einsum(
            "skt,skd->std",
            pick,
            slots.reshape(n_e, capacity, width),
            preferred_element_type=F32,
        ).astype(BF)

    e_rows = take(n2_all)
    e_cot = take(cot_all[:, :tokens]).astype(F32)
    e_logits = mm(e_rows, router)
    expert_ids = jnp.arange(n_experts, dtype=F32)[None, :]
    e_diff = jnp.sum(
        jnp.where(expert_ids == me.astype(F32), e_logits, 0.0)
        - jnp.where(expert_ids == other_slot.reshape(-1, 1), e_logits, 0.0),
        axis=1,
        keepdims=True,
    )
    e_gates = jax.nn.sigmoid(e_diff)
    ge = mm(e_rows, e_gate)
    ue = mm(e_rows, e_up)
    inner = (ge * jax.nn.sigmoid(ge) * ue).astype(BF)
    result = mm(inner, e_down).astype(BF).astype(F32)
    c = (e_gates * e_cot).astype(BF)
    dge, due = gated_backward(ge, ue, mm_tr(c, e_down))
    b = (mm_tr(dge, e_gate) + mm_tr(due, e_up)).astype(BF)
    dgate_slot = jnp.sum(e_cot * result, axis=-1).reshape(n_e, 1, capacity)
    high = lax.reduce_precision(dgate_slot, 8, 7)
    low = (dgate_slot - high).astype(BF)
    pair = jnp.concatenate([high.astype(BF), low], axis=1)
    dgate_rows = jnp.einsum("sik,skt->sit", pair, pick, preferred_element_type=F32)
    dgate_rows = jnp.where(mine[:, :, None, :], dgate_rows[:, None], 0.0).astype(BF)
    dgate_rows = jnp.pad(
        dgate_rows.reshape(n_e, 4, tokens), ((0, 0), (0, 12), (0, width - tokens))
    )
    b_back = lax.psum_scatter(
        jnp.concatenate([put(b), dgate_rows], axis=1), "expert", scatter_dimension=0
    )
    y_back = lax.psum_scatter(
        put((e_gates * result).astype(BF)), "expert", scatter_dimension=0
    ).astype(F32)

    def reduce_fsdp(full):
        parts = full.astype(BF).reshape(n_f, full.shape[0] // n_f, full.shape[1])
        parts = lax.all_to_all(parts, "fsdp", split_axis=0, concat_axis=0, tiled=True)
        return jnp.sum(parts.astype(F32), axis=0)[None]

    grad_e_down = reduce_fsdp(mm_tl(inner, c))
    grad_e_gate = reduce_fsdp(mm_tl(e_rows, dge))
    grad_e_up = reduce_fsdp(mm_tl(e_rows, due))

    sg = mm(n2, s_gate)
    su = mm(n2, s_up)
    sh = (sg * jax.nn.sigmoid(sg) * su).astype(BF)
    shared_result = mm(sh, s_down)
    gy = cotangent.astype(F32)
    dsg, dsu = gated_backward(sg, su, mm_tr(cotangent, s_down))
    shared_grads = lax.psum_scatter(
        jnp.concatenate(
            [
                split_chunks(mm_tl(n2, dsg).astype(BF), n_all),
                split_chunks(mm_tl(n2, dsu).astype(BF), n_all),
                split_chunks(mm_tl(sh, cotangent).astype(BF), n_all),
            ],
            axis=1,
        ),
        ALL,
        scatter_dimension=0,
    ).astype(F32)
    grad_s_gate = from_chunks(shared_grads[None, :per], rows, hidden)
    grad_s_up = from_chunks(shared_grads[None, per : 2 * per], rows, hidden)
    grad_s_down = from_chunks(shared_grads[None, 2 * per :], down_rows, width)
    output = (h + y_back + shared_result).astype(BF)

    logits = mm(n2, router)
    ids = jnp.arange(n_experts, dtype=jnp.int32)
    onehot = (routes[:, :, None] == ids).astype(F32)
    chosen = jnp.sum(logits[:, None, :] * onehot, axis=-1)
    gates = jax.nn.softmax(chosen, axis=-1)
    returned = b_back[tokens : tokens + 4, :tokens].astype(F32)
    dgate = (returned[0::2] + returned[1::2]).T
    dchosen = gates * (dgate - jnp.sum(gates * dgate, axis=-1, keepdims=True))
    dlogits = jnp.sum(dchosen[:, :, None] * onehot, axis=1).astype(BF)
    grad_router = mm_tl(n2, dlogits)
    dn2 = (
        mm_tr(dsg, s_gate)
        + mm_tr(dsu, s_up)
        + mm_tr(dlogits, router)
        + b_back[:tokens].astype(F32)
    )
    grad_h, grad_gain_two = norm_backward(h, r2, gain_two, dn2)
    dh = gy + grad_h

    da = dh.astype(BF)
    grad_w_o = mm_tl(mix, da)
    grad_mix = mm_tr(da, w_o).astype(BF).reshape(heads)
    dqr, dkr, dvv = attention_backward(query, key, value, grad_mix, probs)
    dq = rotate(dqr, cosine, -sine).astype(BF).reshape(tokens, width)
    dk = rotate(dkr, cosine, -sine).astype(BF).reshape(tokens, width)
    dv = dvv.astype(BF).reshape(tokens, width)
    dn1 = mm_tr(dq, w_q) + mm_tr(dk, w_k) + mm_tr(dv, w_v)
    grad_x, grad_gain_one = norm_backward(x, r1, gain_one, dn1)
    grad_hidden = dh + grad_x

    small = jnp.concatenate(
        [
            grad_gain_one.reshape(n_all, rows),
            grad_gain_two.reshape(n_all, rows),
            grad_router.reshape(n_all, rows * n_experts),
        ],
        axis=1,
    )
    small = jnp.pad(small, ((0, 0), (0, 8 * width - small.shape[1]))).reshape(n_all, 8, width)
    dense = [mm_tl(n1, dq), mm_tl(n1, dk), mm_tl(n1, dv), grad_w_o]
    dense = [item.reshape(n_all, rows, width) for item in dense] + [small]
    dense = lax.psum_scatter(
        jnp.concatenate([item.astype(BF) for item in dense], axis=1), ALL, scatter_dimension=0
    ).astype(F32)
    last = dense[4 * rows]
    return (
        output,
        grad_hidden,
        last[:rows],
        dense[:rows],
        dense[rows : 2 * rows],
        dense[2 * rows : 3 * rows],
        dense[3 * rows : 4 * rows],
        last[rows : 2 * rows],
        last[2 * rows : (2 + n_experts) * rows].reshape(rows, n_experts),
        grad_s_gate,
        grad_s_up,
        grad_s_down,
        grad_e_gate,
        grad_e_up,
        grad_e_down,
    )


def solution(mesh):
    row = P(ALL, None)
    vector = P(ALL)
    expert = P("expert", "fsdp", None)
    return jax.shard_map(
        functools.partial(per_device, n_e=mesh.shape["expert"], n_f=mesh.shape["fsdp"]),
        mesh=mesh,
        in_specs=(
            (row, row, vector, row, row, row, row, vector)
            + (row, row, row, row, expert, expert, expert, row)
        ),
        out_specs=(
            (row, row, vector, row, row, row, row, vector)
            + (row, row, row, row, expert, expert, expert)
        ),
        check_vma=False,
    )
```

time: 1590 us -> 934 us (0.59)
  waiting for transfers between devices: 980 us -> 527 us
  blocking collectives: 206 us -> 0 us
  matrix products: 236 us -> 210 us
  local copies, waits for them, and re-layouts: 83.8 us -> 103 us
    reduce_scatter x10 -> x4, waiting for transfers between devices: 607 us -> 228 us  [the longest x1 108 us: per_device(): lax.psum_scatter(jnp.concatenate([item.astype(BF) for item in dense], axi...]
    ppermute x0 -> x13, waiting for transfers between devices: none -> 166 us  [the longest x3 89.2 us: gather_expert(): part = lax.ppermute(block, 'expert', [(i, i ^ 2 * k) for i in range(n_e)])]
    all_gather x1 -> x0, blocking collectives: 126 us -> none  [per_device(): lax.all_gather(w_router, ('expert', 'fsdp'), axis=0, tiled=True)]
    all_gather x10 -> x3, waiting for transfers between devices: 186 us -> 64.7 us  [the longest x1 64.6 us: per_device(): lax.all_gather(jnp.concatenate([w_query, w_key, w_value, w_output, extras...]
    all_to_all x4 -> x3, waiting for transfers between devices: 181 us -> 67.4 us  [reduce_fsdp(): lax.all_to_all(parts, 'fsdp', split_axis=0, concat_axis=0, tiled=True)]
    unnamed x2 -> x0, blocking collectives: 79.5 us -> none
    gather x9 -> x0, local copies, waits for them, and re-layouts: 36.5 us -> none  [the longest x1 9.41 us: per_device(): outgoing = padded_rows[owner_token].reshape(expert_count, capacity, width)]
    dot_general x42 -> x51, matrix products: 236 us -> 202 us  [the longest x35 171 us: dot(): lax.dot_general(left, right, (contract, ((), ())), preferred_element_type...]
  transfers between devices with their start and end apart: 24 -> 23, of which waited for: 14 -> 13; matrix products, arithmetic and copies ran while one was open for 22% -> 32% of each run, Pallas kernels for 0% -> 0%
where the time goes in v1:
time: 934 us; the launch traced here: 923 us
  waiting for transfers between devices  527 us (56%)
  matrix products  210 us (22%)
  local copies, waits for them, and re-layouts  103 us (11%)
  other arithmetic  36.8 us (4%)
  starting transfers between devices  30.2 us (3%)
  between operations  16 us (2%)
    dot_general x35, matrix products, dot(): lax.dot_general(left, right, (contract, ((), ())), preferred_element_type...  171 us
    reduce_scatter x1, waiting for transfers between devices, per_device(): lax.psum_scatter(jnp.concatenate([item.astype(BF) for item in dense], axi...  108 us
    ppermute x3, waiting for transfers between devices, gather_expert(): part = lax.ppermute(block, 'expert', [(i, i ^ 2 * k) for i in range(n_e)])  89.2 us
    ppermute x9, waiting for transfers between devices, gather_fsdp(): part = lax.ppermute(block, 'fsdp', [(i, i ^ k) for i in range(n_f)])  77.2 us
    reduce_scatter x1, waiting for transfers between devices, per_device(): lax.psum_scatter(put((e_gates * result).astype(BF)), 'expert', scatter_di...  67.5 us
    all_to_all x3, waiting for transfers between devices, reduce_fsdp(): lax.all_to_all(parts, 'fsdp', split_axis=0, concat_axis=0, tiled=True)  67.4 us
    all_gather x1, waiting for transfers between devices, per_device(): lax.all_gather(jnp.concatenate([w_query, w_key, w_value, w_output, extras...  64.6 us
    reduce_scatter x1, waiting for transfers between devices, per_device(): lax.psum_scatter(jnp.concatenate([split_chunks(mm_tl(n2, dsg).astype(BF),...  30 us
  transfers between devices with their start and end apart: 23, of which 13 were waited for; matrix products, arithmetic and copies ran while one was open for 32% of the time, Pallas kernels for 0%

profile of v1, /device:TPU:0, one launch (start us, length us, event | category | flops | bytes accessed | tf_op | source)
XLA Modules:
  0.0 923.5 jit_solution(4412083119709118363)
XLA Ops:
  15.7 64.6 %all-gather.7.cloned.1.call-done = bf16[3328,768]{1,0:T(8,128)(2,1)} async-done(((bf16[104,768]{1,0:T(8,128)(2,1)}), bf16[3328,768]{1,0:T(8,128)(2,1)}) %all-gather.7.cloned.1.call-update) | async-done | bytes 5111824 | tf_op jit(solution)/shard_map/all_gather | solution.py:197
  81.4 4.1 fusion.149
  85.7 3.3 copy.162
  90.4 2.3 fusion.94
  94.2 3.4 fusion.154
  97.6 5.2 fusion.153
  104.9 2.5 convolution_convert_fusion.13
  107.5 4.1 fusion.85
  124.5 56.2 %collective-permute-done = bf16[528,768]{1,0:T(8,128)(2,1)} collective-permute-done((bf16[528,768]{1,0:T(8,128)(2,1)}, bf16[528,768]{1,0:T(8,128)(2,1)}, u32[]{:S(2)}, u32[]{:S(2)}) %collective-permute-start) | collective-permute-done | bytes 811040 | tf_op jit(solution)/shard_map/ppermute | solution.py:109
  183.3 7.7 collective-permute-done.1
  193.7 25.2 %collective-permute-done.2 = bf16[528,768]{1,0:T(8,128)(2,1)} collective-permute-done((bf16[528,768]{1,0:T(8,128)(2,1)}, bf16[528,768]{1,0:T(8,128)(2,1)}, u32[]{:S(2)}, u32[]{:S(2)}) %collective-permute-start.2) | collective-permute-done | bytes 811040 | tf_op jit(solution)/shard_map/ppermute | solution.py:109
  225.2 2.1 constant_dynamic-update-slice_fusion.18
  229.2 2.1 constant_dynamic-update-slice_fusion.10
  232.0 2.2 collective-permute-start.8
  234.3 2.1 constant_dynamic-update-slice_fusion.13
  236.4 2.1 constant_dynamic-update-slice_fusion.17
  240.6 2.1 constant_dynamic-update-slice_fusion.9
  242.7 2.1 constant_dynamic-update-slice_fusion.8
  244.8 9.3 %collective-permute-done.12 = bf16[512,768]{1,0:T(8,128)(2,1)} collective-permute-done((bf16[512,768]{1,0:T(8,128)(2,1)}, bf16[512,768]{1,0:T(8,128)(2,1)}, u32[]{:S(2)}, u32[]{:S(2)}) %collective-permute-start.12) | collective-permute-done | bytes 786464 | tf_op jit(solution)/shard_map/ppermute | solution.py:97
  255.2 2.1 constant_dynamic-update-slice_fusion.7
  257.3 47.8 %collective-permute-done.8 = bf16[192,2048]{1,0:T(8,128)(2,1)S(1)} collective-permute-done((bf16[192,2048]{1,0:T(8,128)(2,1)}, bf16[192,2048]{1,0:T(8,128)(2,1)S(1)}, u32[]{:S(2)}, u32[]{:S(2)}) %collective-permute-start.8) | collective-permute-done | bytes 786464 | tf_op jit(solution)/shard_map/ppermute | solution.py:97
  306.0 20.1 %collective-permute-done.5 = bf16[192,2048]{1,0:T(8,128)(2,1)S(1)} collective-permute-done((bf16[192,2048]{1,0:T(8,128)(2,1)}, bf16[192,2048]{1,0:T(8,128)(2,1)S(1)}, u32[]{:S(2)}, u32[]{:S(2)}) %collective-permute-start.5) | collective-permute-done | bytes 786464 | tf_op jit(solution)/shard_map/ppermute | solution.py:97
  329.8 2.3 bitcast_dynamic-update-slice_fusion.1
  336.3 4.6 fusion.39
  342.7 12.6 %fusion.159 = f32[2048,2048]{1,0:T(8,128)} fusion(bf16[2048,768]{1,0:T(8,128)(2,1)S(1)} %bitcast.324, bf16[768,2048]{1,0:T(8,128)(2,1)} %constant_dynamic-update-slice_fusion.11), kind=kOutput, calls=%fused_computation.270 | convolution fusion | flops 6442450944 | bytes 23068672 | tf_op jit(solution)/shard_map/dot_general | solution.py:35
  355.3 11.4 %fusion.165 = f32[2048,2048]{1,0:T(8,128)} fusion(bf16[2048,768]{1,0:T(8,128)(2,1)S(1)} %fusion.6, bf16[2048,768]{1,0:T(8,128)(2,1)} %constant_dynamic-update-slice_fusion.7), kind=kOutput, calls=%fused_computation.276 | convolution fusion | flops 6442450944 | bytes 23068672 | tf_op jit(solution)/shard_map/dot_general | solution.py:35
  366.7 28.1 %multiply_convert_fusion.1 = (bf16[2048,2048]{1,0:T(8,128)(2,1)}, bf16[2048,2048]{1,0:T(8,128)(2,1)}, bf16[2048,2048]{1,0:T(8,128)(2,1)}) fusion(f32[2048,2048]{1,0:T(8,128)} %fusion.165, f32[2048,2048]{1,0:T(8,128)} %fusion.159, bf16[2048,768]{1,0:T(8,128)(2,1)} %bitcast.325, bf16[768,2048]{1,0:T(8,128)(2,1)} %constant_dynamic-update-slice_fusion.15), kind=kOutput, calls=%fused_computation.3 | convolution fusion | flops 6505365504 | bytes 65011712 | tf_op jit(solution)/shard_map/dot_general | solution.py:35
  394.8 11.3 %fusion.7 = (f32[2048]{0:T(1024)S(1)}, bf16[2048,768]{1,0:T(8,128)(2,1)}) fusion(bf16[8,256,768]{2,1,0:T(8,128)(2,1)S(1)} %fusion.42, f32[2048]{0:T(1024)S(1)} %add_divide_fusion.2, bf16[2048,2048]{1,0:T(8,128)(2,1)} %get-tuple-element.100, bf16[2048,768]{1,0:T(8,128)(2,1)} %constant_dynamic-update-slice_fusion.7), kind=kOutput, calls=%fused_computation.16 | convolution fusion | flops 6453458944 | bytes 17842176 | tf_op jit(solution)/shard_map/dot_general | solution.py:35
  407.2 10.3 %fusion.166 = f32[2048,768]{1,0:T(8,128)S(1)} fusion(bf16[2048,2048]{1,0:T(8,128)(2,1)} %get-tuple-element.99, bf16[768,2048]{1,0:T(8,128)(2,1)} %constant_dynamic-update-slice_fusion.11), kind=kOutput, calls=%fused_computation.277 | convolution fusion | flops 6442450944 | bytes 17825792 | tf_op jit(solution)/shard_map/dot_general | solution.py:35
  417.5 10.1 %add_convert_fusion = bf16[2048,768]{1,0:T(8,128)(2,1)S(1)} fusion(f32[2048,768]{1,0:T(8,128)S(1)} %fusion.166, bf16[2048,2048]{1,0:T(8,128)(2,1)} %get-tuple-element.98, bf16[768,2048]{1,0:T(8,128)(2,1)} %constant_dynamic-update-slice_fusion.15), kind=kOutput, calls=%fused_computation.24 | convolution fusion | flops 6445596672 | bytes 20971520 | tf_op jit(solution)/shard_map/dot_general | solution.py:35
  429.5 3.2 fusion.4
  432.8 4.4 fusion.148
  441.5 3.0 copy.172
  449.3 3.9 fusion.15
  460.2 2.7 copy.187
  462.9 3.5 convolution_convert_fusion.3
  466.4 9.4 %reshape.452 = bf16[32,64,3,256]{3,2,1,0:T(4,128)(2,1)} reshape(bf16[2048,768]{1,0:T(8,128)(2,1)} %convolution_convert_fusion.3) | data formatting | bytes 6291456 | tf_op jit(solution)/shard_map/reshape | solution.py:83
  475.8 3.1 copy.188
  478.9 4.2 pad_maximum_fusion
  485.1 5.0 fusion.162
  490.1 3.0 fusion.163
  493.1 4.6 fusion.29
  499.6 10.5 %convolution_convert_fusion.6 = bf16[2048,768]{1,0:T(8,128)(2,1)} fusion(bf16[2048,2048]{1,0:T(8,128)(2,1)} %get-tuple-element.100, bf16[2048,768]{1,0:T(8,128)(2,1)S(1)} %copy-done.25), kind=kOutput, calls=%fused_computation.57 | convolution fusion | flops 6444023808 | bytes 14680064 | tf_op jit(solution)/shard_map/dot_general | solution.py:35
  510.1 4.9 all-to-all-start.2
  515.0 22.3 %reduce-scatter.7.cloned.1.call-done = bf16[1,528,768]{2,1,0:T(8,128)(2,1)} async-done(((bf16[8,528,768]{2,1,0:T(8,128)(2,1)}), bf16[1,528,768]{2,1,0:T(8,128)(2,1)}) %reduce-scatter.7.cloned.1.call-update) | async-done | bytes 811024 | tf_op jit(solution)/shard_map/reduce_scatter | solution.py:292
  538.2 3.1 multiply_reduce_fusion.4
  547.1 3.1 multiply_reduce_fusion.2
  553.9 2.3 multiply_reduce_fusion
  564.8 2.3 fusion.68
  570.3 3.8 fusion.143
  574.1 2.3 copy.181
  586.5 12.3 %convolution_convert_fusion.1 = bf16[768,2048]{1,0:T(8,128)(2,1)} fusion(bf16[2048,768]{1,0:T(8,128)(2,1)} %bitcast.326, bf16[2048,2048]{1,0:T(8,128)(2,1)} %get-tuple-element.98), kind=kOutput, calls=%fused_computation.52 | convolution fusion | flops 6444023808 | bytes 14680064 | tf_op jit(solution)/shard_map/dot_general | solution.py:35
  598.7 4.7 all-to-all-start
  603.4 12.1 %convolution_convert_fusion = bf16[768,2048]{1,0:T(8,128)(2,1)} fusion(bf16[2048,768]{1,0:T(8,128)(2,1)} %bitcast.327, bf16[2048,2048]{1,0:T(8,128)(2,1)} %get-tuple-element.99), kind=kOutput, calls=%fused_computation.51 | convolution fusion | flops 6444023808 | bytes 14680064 | tf_op jit(solution)/shard_map/dot_general | solution.py:35
  615.5 30.8 %all-to-all-done = bf16[4,192,2048]{2,1,0:T(8,128)(2,1)} async-done(((bf16[4,192,2048]{2,1,0:T(8,128)(2,1)}), bf16[4,192,2048]{2,1,0:T(8,128)(2,1)}, u32[]{:S(2)}, u32[]{:S(2)}) %all-to-all-start) | async-done | bytes 3145760 | tf_op jit(solution)/shard_map/all_to_all | solution.py:301
  646.2 4.6 all-to-all-start.1
  650.9 3.6 convert_reduce_fusion
  654.5 3.8 convert_reduce_fusion.2
  658.3 36.7 %all-to-all-done.1 = bf16[4,192,2048]{2,1,0:T(8,128)(2,1)} async-done(((bf16[4,192,2048]{2,1,0:T(8,128)(2,1)}), bf16[4,192,2048]{2,1,0:T(8,128)(2,1)}, u32[]{:S(2)}, u32[]{:S(2)}) %all-to-all-start.1) | async-done | bytes 3145760 | tf_op jit(solution)/shard_map/all_to_all | solution.py:301
  695.0 3.8 convert_reduce_fusion.1
  698.7 30.0 %reduce-scatter.11.cloned.1.call-done = bf16[1,576,256]{2,1,0:T(8,128)(2,1)} async-done(((bf16[32,576,256]{2,1,0:T(8,128)(2,1)}), bf16[1,576,256]{2,1,0:T(8,128)(2,1)}) %reduce-scatter.11.cloned.1.call-update) | async-done | bytes 294928 | tf_op jit(solution)/shard_map/reduce_scatter | solution.py:314
  732.0 67.5 %reduce-scatter.5.cloned.1.call-done = bf16[1,512,768]{2,1,0:T(8,128)(2,1)} async-done(((bf16[8,512,768]{2,1,0:T(8,128)(2,1)}), bf16[1,512,768]{2,1,0:T(8,128)(2,1)}) %reduce-scatter.5.cloned.1.call-update) | async-done | bytes 786448 | tf_op jit(solution)/shard_map/reduce_scatter | solution.py:295
  799.5 5.4 fusion.70
  804.9 108.2 %reduce-scatter.9.cloned.1.call-done = bf16[1,104,768]{2,1,0:T(8,128)(2,1)} async-done(((bf16[32,104,768]{2,1,0:T(8,128)(2,1)}), bf16[1,104,768]{2,1,0:T(8,128)(2,1)}) %reduce-scatter.9.cloned.1.call-update) | async-done | bytes 159760 | tf_op jit(solution)/shard_map/reduce_scatter | solution.py:372
  (353 shorter events, 115.9 us)
Async XLA Ops:
  7.2 73.1 %all-gather.7.cloned.1.call-start = ((), (), s32[]{:S(2)}) async-start(), calls=%async_computation.11 | async-start | bytes 5271552 | tf_op jit(solution)/shard_map/all_gather | solution.py:197
  12.7 323.6 %all-gather.9.cloned.1.call-start = ((), (), s32[]{:S(2)}) async-start(), calls=%async_computation.12 | async-start | bytes 7077888 | tf_op jit(solution)/shard_map/all_gather | solution.py:237
  14.7 78.0 %copy-start.74 = (f32[512]{0:T(512)}, f32[512]{0:T(512)S(1)}, u32[]{:S(2)}) copy-start(f32[512]{0:T(512)S(1)} %get-tuple-element.145) | copy-start | bytes 6148
  85.5 7.2 copy-start.12
  85.5 17.4 %copy-start.10 = (bf16[32,24,768]{2,1,0:T(8,128)(2,1)}, bf16[32,24,768]{2,1,0:T(8,128)(2,1)S(1)}, u32[]{:S(2)}) copy-start(bf16[32,24,768]{2,1,0:T(8,128)(2,1)S(1)} %get-tuple-element.110) | copy-start | bytes 3538948
  85.5 4.9 copy-start.8
  85.5 7.2 copy-start.60
  85.7 7.0 copy-start.66
  90.4 3.2 copy-start.58
  94.2 8.6 copy-start.15
  94.2 8.6 copy-start.17
  94.2 8.6 copy-start.19
  94.2 8.6 copy-start.21
  107.5 4.1 copy-start.51
  107.5 4.1 copy-start.35
  112.5 10.2 %copy-start = (f32[512,768]{1,0:T(8,128)}, f32[512,768]{1,0:T(8,128)S(1)}, u32[]{:S(2)}) copy-start(f32[512,768]{1,0:T(8,128)S(1)} %get-tuple-element.156) | copy-start | bytes 4718596
  112.6 9.2 copy-start.61
  112.6 9.3 %copy-start.62 = (bf16[24,2048]{1,0:T(8,128)(2,1)S(1)}, bf16[24,2048]{1,0:T(8,128)(2,1)}, u32[]{:S(2)}) copy-start(bf16[24,2048]{1,0:T(8,128)(2,1)} %param.25) | copy-start | bytes 294916
  112.6 9.3 %copy-start.63 = (bf16[24,2048]{1,0:T(8,128)(2,1)S(1)}, bf16[24,2048]{1,0:T(8,128)(2,1)}, u32[]{:S(2)}) copy-start(bf16[24,2048]{1,0:T(8,128)(2,1)} %param.26) | copy-start | bytes 294916
  113.2 9.6 %copy-start.72 = (f32[512]{0:T(512)}, f32[512]{0:T(512)S(1)}, u32[]{:S(2)}) copy-start(f32[512]{0:T(512)S(1)} %get-tuple-element.147) | copy-start | bytes 6148
  113.2 9.5 %copy-start.64 = (f32[768]{0:T(1024)}, f32[768]{0:T(1024)S(1)}, u32[]{:S(2)}) copy-start(f32[768]{0:T(1024)S(1)} %reshape.461) | copy-start | bytes 9220
  114.4 318.5 %all-gather.11.cloned.1.call-start = ((), (), s32[]{:S(2)}) async-start(), calls=%async_computation.13 | async-start | bytes 9732096 | tf_op jit(solution)/shard_map/all_gather | solution.py:208
  115.4 65.3 %collective-permute-start = (bf16[528,768]{1,0:T(8,128)(2,1)}, bf16[528,768]{1,0:T(8,128)(2,1)}, u32[]{:S(2)}, u32[]{:S(2)}) collective-permute-start(bf16[528,768]{1,0:T(8,128)(2,1)} %fusion.89), channel_id=1, source_target_pairs={{0,8},{4,12},{8,0},{12,4},{16,24},{20,28},{24,16},{28,20},{1,9},{5... | collective-permute-start | bytes 2433032 | tf_op jit(solution)/shard_map/ppermute | solution.py:109
  117.0 74.0 %collective-permute-start.1 = (bf16[528,768]{1,0:T(8,128)(2,1)}, bf16[528,768]{1,0:T(8,128)(2,1)}, u32[]{:S(2)}, u32[]{:S(2)}) collective-permute-start(bf16[528,768]{1,0:T(8,128)(2,1)} %fusion.89), channel_id=1, source_target_pairs={{0,16},{4,20},{8,24},{12,28},{16,0},{20,4},{24,8},{28,12},{1,17},{... | collective-permute-start | bytes 2433032 | tf_op jit(solution)/shard_map/ppermute | solution.py:109
  117.8 101.1 %collective-permute-start.2 = (bf16[528,768]{1,0:T(8,128)(2,1)}, bf16[528,768]{1,0:T(8,128)(2,1)}, u32[]{:S(2)}, u32[]{:S(2)}) collective-permute-start(bf16[528,768]{1,0:T(8,128)(2,1)} %fusion.89), channel_id=1, source_target_pairs={{0,24},{4,28},{8,16},{12,20},{16,8},{20,12},{24,0},{28,4},{1,25},{... | collective-permute-start | bytes 2433032 | tf_op jit(solution)/shard_map/ppermute | solution.py:109
  119.8 111.5 %collective-permute-start.10 = (bf16[512,768]{1,0:T(8,128)(2,1)}, bf16[512,768]{1,0:T(8,128)(2,1)}, u32[]{:S(2)}, u32[]{:S(2)}) collective-permute-start(bf16[512,768]{1,0:T(8,128)(2,1)} %bitcast.31), channel_id=1, source_target_pairs={{0,1},{1,0},{2,3},{3,2},{4,5},{5,4},{6,7},{7,6},{8,9},{9,8},{10,11... | collective-permute-start | bytes 2359304 | tf_op jit(solution)/shard_map/ppermute | solution.py:97
  121.2 117.4 %collective-permute-start.11 = (bf16[512,768]{1,0:T(8,128)(2,1)}, bf16[512,768]{1,0:T(8,128)(2,1)}, u32[]{:S(2)}, u32[]{:S(2)}) collective-permute-start(bf16[512,768]{1,0:T(8,128)(2,1)} %bitcast.31), channel_id=1, source_target_pairs={{0,2},{1,3},{2,0},{3,1},{4,6},{5,7},{6,4},{7,5},{8,10},{9,11},{10,... | collective-permute-start | bytes 2359304 | tf_op jit(solution)/shard_map/ppermute | solution.py:97
  122.8 414.6 %reduce-scatter.7.cloned.1.call-start = ((), (), s32[]{:S(2)}) async-start(), calls=%async_computation.8 | async-start | bytes 7299072 | tf_op jit(solution)/shard_map/reduce_scatter | solution.py:292
  180.7 51.3 %collective-permute-start.7 = (bf16[192,2048]{1,0:T(8,128)(2,1)}, bf16[192,2048]{1,0:T(8,128)(2,1)}, u32[]{:S(2)}, u32[]{:S(2)}) collective-permute-start(bf16[192,2048]{1,0:T(8,128)(2,1)} %bitcast.345), channel_id=1, source_target_pairs={{0,1},{1,0},{2,3},{3,2},{4,5},{5,4},{6,7},{7,6},{8,9},{9,8},{10,11... | collective-permute-start | bytes 2359304 | tf_op jit(solution)/shard_map/ppermute | solution.py:97
  191.0 31.2 %copy-start.40 = (bf16[1,192,2048]{2,1,0:T(8,128)(2,1)S(1)}, bf16[1,192,2048]{2,1,0:T(8,128)(2,1)}, u32[]{:S(2)}) copy-start(bf16[1,192,2048]{2,1,0:T(8,128)(2,1)} %param.29) | copy-start | bytes 2359300
  191.0 45.4 %collective-permute-start.4 = (bf16[192,2048]{1,0:T(8,128)(2,1)}, bf16[192,2048]{1,0:T(8,128)(2,1)}, u32[]{:S(2)}, u32[]{:S(2)}) collective-permute-start(bf16[192,2048]{1,0:T(8,128)(2,1)} %bitcast.29), channel_id=1, source_target_pairs={{0,1},{1,0},{2,3},{3,2},{4,5},{5,4},{6,7},{7,6},{8,9},{9,8},{10,11... | collective-permute-start | bytes 2359304 | tf_op jit(solution)/shard_map/ppermute | solution.py:97
  220.1 109.7 %collective-permute-start.3 = (bf16[4,528,768]{2,1,0:T(8,128)(2,1)S(1)}, bf16[4,528,768]{2,1,0:T(8,128)(2,1)}, u32[]{:S(2)}, u32[]{:S(2)}) collective-permute-start(bf16[4,528,768]{2,1,0:T(8,128)(2,1)S(1)} %bitcast_dynamic-update-slice_fusion.2), channel_id=1, source_target_pairs={{0,4},{4,0},{8,12},{12,8},{16,20},{20,16},{24,28},{28,24},{1,5},{5... | collective-permute-start | bytes 9732104 | tf_op jit(solution)/shard_map/ppermute | solution.py:111
  231.3 22.8 %collective-permute-start.12 = (bf16[512,768]{1,0:T(8,128)(2,1)}, bf16[512,768]{1,0:T(8,128)(2,1)}, u32[]{:S(2)}, u32[]{:S(2)}) collective-permute-start(bf16[512,768]{1,0:T(8,128)(2,1)} %bitcast.31), channel_id=1, source_target_pairs={{0,3},{1,2},{2,1},{3,0},{4,7},{5,6},{6,5},{7,4},{8,11},{9,10},{10,... | collective-permute-start | bytes 2359304 | tf_op jit(solution)/shard_map/ppermute | solution.py:97
  232.0 6.6 copy-start.41
  232.0 73.0 %collective-permute-start.8 = (bf16[192,2048]{1,0:T(8,128)(2,1)}, bf16[192,2048]{1,0:T(8,128)(2,1)S(1)}, u32[]{:S(2)}, u32[]{:S(2)}) collective-permute-start(bf16[192,2048]{1,0:T(8,128)(2,1)} %bitcast.346), channel_id=1, source_target_pairs={{0,2},{1,3},{2,0},{3,1},{4,6},{5,7},{6,4},{7,5},{8,10},{9,11},{10,... | collective-permute-start | bytes 2359304 | tf_op jit(solution)/shard_map/ppermute | solution.py:97
  236.4 89.7 %collective-permute-start.5 = (bf16[192,2048]{1,0:T(8,128)(2,1)}, bf16[192,2048]{1,0:T(8,128)(2,1)S(1)}, u32[]{:S(2)}, u32[]{:S(2)}) collective-permute-start(bf16[192,2048]{1,0:T(8,128)(2,1)} %bitcast.29), channel_id=1, source_target_pairs={{0,2},{1,3},{2,0},{3,1},{4,6},{5,7},{6,4},{7,5},{8,10},{9,11},{10,... | collective-permute-start | bytes 2359304 | tf_op jit(solution)/shard_map/ppermute | solution.py:97
  238.6 88.5 %collective-permute-start.9 = (bf16[192,2048]{1,0:T(8,128)(2,1)S(1)}, bf16[192,2048]{1,0:T(8,128)(2,1)S(1)}, u32[]{:S(2)}, u32[]{:S(2)}) collective-permute-start(bf16[192,2048]{1,0:T(8,128)(2,1)S(1)} %bitcast.347), channel_id=1, source_target_pairs={{0,3},{1,2},{2,1},{3,0},{4,7},{5,6},{6,5},{7,4},{8,11},{9,10},{10,... | collective-permute-start | bytes 2359304 | tf_op jit(solution)/shard_map/ppermute | solution.py:97
  254.1 74.0 %collective-permute-start.6 = (bf16[192,2048]{1,0:T(8,128)(2,1)}, bf16[192,2048]{1,0:T(8,128)(2,1)S(1)}, u32[]{:S(2)}, u32[]{:S(2)}) collective-permute-start(bf16[192,2048]{1,0:T(8,128)(2,1)} %bitcast.29), channel_id=1, source_target_pairs={{0,3},{1,2},{2,1},{3,0},{4,7},{5,6},{6,5},{7,4},{8,11},{9,10},{10,... | collective-permute-start | bytes 2359304 | tf_op jit(solution)/shard_map/ppermute | solution.py:97
  336.2 4.7 copy-start.32
  342.7 12.6 %copy-start.24 = (bf16[2048,768]{1,0:T(8,128)(2,1)}, bf16[2048,768]{1,0:T(8,128)(2,1)S(1)}, u32[]{:S(2)}) copy-start(bf16[2048,768]{1,0:T(8,128)(2,1)S(1)} %fusion.6) | copy-start | bytes 9437188
  432.8 295.9 %reduce-scatter.11.cloned.1.call-start = ((), (), s32[]{:S(2)}) async-start(), calls=%async_computation.10 | async-start | bytes 9732096 | tf_op jit(solution)/shard_map/reduce_scatter | solution.py:314
  439.4 6.0 copy-start.26
  441.5 6.0 copy-start.27
  445.3 4.0 copy-start.23
  453.3 4.0 copy-start.82
  453.3 9.6 %copy-start.86 = (bf16[512,2048]{1,0:T(8,128)(2,1)}, bf16[512,2048]{1,0:T(8,128)(2,1)S(1)}, u32[]{:S(2)}) copy-start(bf16[512,2048]{1,0:T(8,128)(2,1)S(1)} %get-tuple-element.106) | copy-start | bytes 6291460
  483.2 316.3 %reduce-scatter.5.cloned.1.call-start = ((), (), s32[]{:S(2)}) async-start(), calls=%async_computation.7 | async-start | bytes 7077888 | tf_op jit(solution)/shard_map/reduce_scatter | solution.py:295
  485.1 5.0 copy-start.28
  485.1 5.0 copy-start.83
  510.1 28.1 %copy-start.1 = (f32[512,768]{1,0:T(8,128)S(1)}, f32[512,768]{1,0:T(8,128)}, u32[]{:S(2)}) copy-start(f32[512,768]{1,0:T(8,128)} %copy-done) | copy-start | bytes 4718596
  510.1 28.1 %copy-start.34 = (f32[512,768]{1,0:T(8,128)S(1)}, f32[512,768]{1,0:T(8,128)}, u32[]{:S(2)}) copy-start(f32[512,768]{1,0:T(8,128)} %fusion.162) | copy-start | bytes 4718596
  510.1 28.1 %copy-start.65 = (f32[768]{0:T(1024)S(1)}, f32[768]{0:T(1024)}, u32[]{:S(2)}) copy-start(f32[768]{0:T(1024)} %copy-done.64) | copy-start | bytes 9220
  510.1 28.2 %copy-start.73 = (f32[512]{0:T(512)S(1)}, f32[512]{0:T(512)}, u32[]{:S(2)}) copy-start(f32[512]{0:T(512)} %copy-done.72) | copy-start | bytes 6148
  510.1 88.7 %all-to-all-start.2 = ((bf16[4,512,768]{2,1,0:T(8,128)(2,1)}), bf16[4,512,768]{2,1,0:T(8,128)(2,1)}, u32[]{:S(2)}, u32[]{:S(2)}) async-start(bf16[4,512,768]{2,1,0:T(8,128)(2,1)} %bitcast.314), calls=%async_computation.6 | async-start | bytes 6291456 | tf_op jit(solution)/shard_map/all_to_all | solution.py:301
  515.0 398.1 %reduce-scatter.9.cloned.1.call-start = ((), (), s32[]{:S(2)}) async-start(), calls=%async_computation.9 | async-start | bytes 5271552 | tf_op jit(solution)/shard_map/reduce_scatter | solution.py:372
  547.1 3.4 copy-start.30
  547.1 3.4 copy-start.77
  547.1 6.8 slice-start
  550.5 3.4 slice-start.1
  564.8 4.7 copy-start.81
  570.3 6.2 copy-start.52
  578.5 3.9 copy-start.39
  598.7 47.5 %all-to-all-start = ((bf16[4,192,2048]{2,1,0:T(8,128)(2,1)}), bf16[4,192,2048]{2,1,0:T(8,128)(2,1)}, u32[]{:S(2)}, u32[]{:S(2)}) async-start(bf16[4,192,2048]{2,1,0:T(8,128)(2,1)} %bitcast.320), calls=%async_computation.4 | async-start | bytes 6291456 | tf_op jit(solution)/shard_map/all_to_all | solution.py:301
  646.2 48.7 %all-to-all-start.1 = ((bf16[4,192,2048]{2,1,0:T(8,128)(2,1)}), bf16[4,192,2048]{2,1,0:T(8,128)(2,1)}, u32[]{:S(2)}, u32[]{:S(2)}) async-start(bf16[4,192,2048]{2,1,0:T(8,128)(2,1)} %bitcast.319), calls=%async_computation.5 | async-start | bytes 6291456 | tf_op jit(solution)/shard_map/all_to_all | solution.py:301
  (48 other events, 89.5 us)
Sparse Core Ops, SparseCore 0:
  12.8 67.5 all-gather.6
  114.5 122.8 all-gather.8
  240.8 134.5 all-gather.10
  432.9 104.4 reduce-scatter.6
  543.1 185.5 reduce-scatter.10
  730.8 68.6 reduce-scatter.4
  805.1 107.9 reduce-scatter.8
